TPU v7x, 32 devices: a whole 2x2x4 slice. The times are simulated.
32 devices in a mesh: seq: 8 (over z, y), rep: 4 (over x, core).
Axes of the slice: x: 2, y: 2, z: 4, core: 2. Of those that a mesh axis runs over, the one named last changes fastest.
Arguments:
- queries: bfloat16 [4, 2048, 512], P('rep', 'seq'), may hold values from -6 to 6
- key_vectors: bfloat16 [4, 2048, 128], P('rep', 'seq'), may hold values from -6 to 6
- values: bfloat16 [4, 2048, 128], P('rep', 'seq'), may hold values from -6 to 6
- forget_logit: bfloat16 [4, 4, 2048], P('rep', None, 'seq'), may hold values from 0 to 11
- out_grad: bfloat16 [4, 2048, 512], P('rep', 'seq'), may hold values from -6 to 6
- query_gain: float32 [128], replicated, may hold values from 0.1 to 1.9
- key_gain: float32 [128], replicated, may hold values from 0.1 to 1.9
- lengths: int32 [4, 4], P('rep'), may hold values from 1 to 24, 32 in all within a row
Outputs:
- attention: bfloat16 [4, 2048, 512], P('rep', 'seq')
- query_grad: bfloat16 [4, 2048, 512], P('rep', 'seq')
- key_grad: bfloat16 [4, 2048, 128], P('rep', 'seq')
- value_grad: bfloat16 [4, 2048, 128], P('rep', 'seq')
- forget_grad: float32 [4, 4, 2048], P('rep', None, 'seq')
- norm_gain_grad: float32 [2, 128], replicated
Inputs may be any that keep to these rules, and one draw needn't show every extreme that they name: `lengths`: each row lists the documents of one pack in order, in tiles of 64 tokens, and sums to 32.
All inputs are finite; a program needn't handle non-finite values.
Results may differ from a plain program's by a relative error of at most 0.02.
Values may be sent and summed in bfloat16 or wider, within the bound.
No kernel may reach another device: no remote copies, remote signals or barrier semaphores. Data moves between devices by JAX's collectives and lax.ppermute only.
A program may use at most 64 MiB of HBM per device.

v0:
```python
import jax
import jax.numpy as jnp
from jax import lax
from jax.sharding import PartitionSpec as P

TILE = 64
norm_eps = 1e-06
key_span = 512


def shifted(value, axis, steps):
    count = lax.axis_size(axis)
    initial, last = (max(0, -steps), min(count, count - steps))
    return lax.ppermute(value, axis, [(source, source + steps) for source in range(initial, last)])


def norm_rows(raw_values, gain_vec, factor):
    lifted = raw_values.astype(jnp.float32)
    mean_square = jnp.mean(lifted * lifted, axis=-1, keepdims=True)
    return lifted * lax.rsqrt(mean_square + norm_eps) * (gain_vec * factor)


def tile_starts(lengths_row, tile_count):
    doc_ends = jnp.cumsum(lengths_row)
    tile_index = jnp.arange(tile_count, dtype=jnp.int32)
    passed = doc_ends[None, :] <= tile_index[:, None]
    return jnp.sum(jnp.where(passed, lengths_row[None, :], 0), axis=1)


def pad_rows(array_in, along):
    widths = [(0, 0)] * array_in.ndim
    widths[along] = (0, key_span)
    return jnp.pad(array_in, widths)


def prepare(gathered):
    key_all, value_all, logit_all = gathered
    gate = jnp.cumsum(jax.nn.log_sigmoid(logit_all.astype(jnp.float32)), axis=1)
    return (pad_rows(key_all, 0), pad_rows(value_all, 0), pad_rows(gate, 1))


def contract_last(left_rows, right_rows):
    return lax.dot_general(
        left_rows, right_rows, (((1,), (1,)), ((), ())), preferred_element_type=jnp.float32
    )


def contract_first(left_rows, right_rows):
    return lax.dot_general(
        left_rows, right_rows, (((0,), (0,)), ((), ())), preferred_element_type=jnp.float32
    )


def block_scores(
    query_rows, key_pad, gate_pad, query_gate, block_first, tile_first, doc_first, head_count
):
    key_block = lax.dynamic_slice_in_dim(key_pad, block_first, key_span, 0)
    scores = contract_last(query_rows, key_block)
    row_count = query_rows.shape[0] // head_count
    scores = scores.reshape(head_count, row_count, key_span)
    key_gate = lax.dynamic_slice_in_dim(gate_pad, block_first, key_span, 1)
    scores = scores + query_gate[:, :, None] - key_gate[:, None, :]
    key_place = block_first + jnp.arange(key_span, dtype=jnp.int32)
    query_place = tile_first + jnp.arange(row_count, dtype=jnp.int32)
    allowed = (key_place[None, :] >= doc_first) & (key_place[None, :] <= query_place[:, None])
    return (jnp.where(allowed[None, :, :], scores, -jnp.inf), key_block)


def query_setup(query_tile, tile_id, doc_tile, gate_pad, query_gain, head_count, head_dim):
    row_count = query_tile.shape[0]
    scale_factor = head_dim ** (-0.5)
    normed = norm_rows(
        query_tile.reshape(row_count, head_count, head_dim), query_gain, scale_factor
    ).astype(jnp.bfloat16)
    query_rows = normed.transpose(1, 0, 2).reshape(head_count * row_count, head_dim)
    tile_first = tile_id * row_count
    doc_first = doc_tile * row_count
    query_gate = lax.dynamic_slice_in_dim(gate_pad, tile_first, row_count, 1)
    block_count = (tile_first + row_count - doc_first + key_span - 1) // key_span
    return (query_rows, tile_first, doc_first, query_gate, block_count)


def forward_task(
    query_tile, tile_id, doc_tile, key_pad, value_pad, gate_pad, query_gain, head_count
):
    row_count, full_width = query_tile.shape
    head_dim = key_pad.shape[1]
    query_rows, tile_first, doc_first, query_gate, block_count = query_setup(
        query_tile, tile_id, doc_tile, gate_pad, query_gain, head_count, head_dim
    )

    def block_step(block_index, loop_state):
        row_total, value_sum = loop_state
        block_first = doc_first + block_index * key_span
        scores, key_block = block_scores(
            query_rows,
            key_pad,
            gate_pad,
            query_gate,
            block_first,
            tile_first,
            doc_first,
            head_count,
        )
        weights = jnp.exp(scores)
        value_block = lax.dynamic_slice_in_dim(value_pad, block_first, key_span, 0)
        mixed_rows = jnp.dot(
            weights.reshape(head_count * row_count, key_span).astype(jnp.bfloat16),
            value_block,
            preferred_element_type=jnp.float32,
        )
        return (row_total + jnp.sum(weights, axis=2), value_sum + mixed_rows)

    start_state = (
        jnp.zeros((head_count, row_count), jnp.float32),
        jnp.zeros((head_count * row_count, head_dim), jnp.float32),
    )
    row_total, value_sum = lax.fori_loop(0, block_count, block_step, start_state)
    result = value_sum.reshape(head_count, row_count, head_dim) / row_total[:, :, None]
    return result.transpose(1, 0, 2).reshape(row_count, full_width).astype(jnp.bfloat16)


def backward_task(
    partials,
    query_tile,
    grad_tile,
    out_tile,
    tile_id,
    doc_tile,
    key_pad,
    value_pad,
    gate_pad,
    query_gain,
    head_count,
):
    row_count, full_width = query_tile.shape
    head_dim = key_pad.shape[1]
    query_rows, tile_first, doc_first, query_gate, block_count = query_setup(
        query_tile, tile_id, doc_tile, gate_pad, query_gain, head_count, head_dim
    )
    grad_rows = (
        grad_tile.reshape(row_count, head_count, head_dim)
        .transpose(1, 0, 2)
        .reshape(head_count * row_count, head_dim)
    )
    product = grad_tile.astype(jnp.float32) * out_tile.astype(jnp.float32)
    out_inner = jnp.sum(product.reshape(row_count, head_count, head_dim), axis=2).T

    def total_step(block_index, row_total):
        block_first = doc_first + block_index * key_span
        scores, key_block = block_scores(
            query_rows,
            key_pad,
            gate_pad,
            query_gate,
            block_first,
            tile_first,
            doc_first,
            head_count,
        )
        return row_total + jnp.sum(jnp.exp(scores), axis=2)

    row_total = lax.fori_loop(
        0, block_count, total_step, jnp.zeros((head_count, row_count), jnp.float32)
    )

    def grad_step(block_index, loop_state):
        key_part, value_part, gate_part, query_grad, row_sum = loop_state
        block_first = doc_first + block_index * key_span
        scores, key_block = block_scores(
            query_rows,
            key_pad,
            gate_pad,
            query_gate,
            block_first,
            tile_first,
            doc_first,
            head_count,
        )
        probability = jnp.exp(scores) / row_total[:, :, None]
        value_block = lax.dynamic_slice_in_dim(value_pad, block_first, key_span, 0)
        prob_grad = contract_last(grad_rows, value_block).reshape(head_count, row_count, key_span)
        score_grad = probability * (prob_grad - out_inner[:, :, None])
        score_low = score_grad.reshape(head_count * row_count, key_span).astype(jnp.bfloat16)
        prob_low = probability.reshape(head_count * row_count, key_span).astype(jnp.bfloat16)
        query_grad = query_grad + jnp.dot(score_low, key_block, preferred_element_type=jnp.float32)
        key_update = contract_first(score_low, query_rows)
        value_update = contract_first(prob_low, grad_rows)
        key_part = lax.dynamic_update_slice_in_dim(
            key_part,
            lax.dynamic_slice_in_dim(key_part, block_first, key_span, 0) + key_update,
            block_first,
            0,
        )
        value_part = lax.dynamic_update_slice_in_dim(
            value_part,
            lax.dynamic_slice_in_dim(value_part, block_first, key_span, 0) + value_update,
            block_first,
            0,
        )
        column_sum = jnp.sum(score_grad, axis=1)
        gate_part = lax.dynamic_update_slice_in_dim(
            gate_part,
            lax.dynamic_slice_in_dim(gate_part, block_first, key_span, 1) - column_sum,
            block_first,
            1,
        )
        return (key_part, value_part, gate_part, query_grad, row_sum + jnp.sum(score_grad, axis=2))

    start_state = (
        partials[0],
        partials[1],
        partials[2],
        jnp.zeros((head_count * row_count, head_dim), jnp.float32),
        jnp.zeros((head_count, row_count), jnp.float32),
    )
    key_part, value_part, gate_part, query_grad, row_sum = lax.fori_loop(
        0, block_count, grad_step, start_state
    )
    gate_part = lax.dynamic_update_slice_in_dim(
        gate_part,
        lax.dynamic_slice_in_dim(gate_part, tile_first, row_count, 1) + row_sum,
        tile_first,
        1,
    )
    query_result = (
        query_grad.reshape(head_count, row_count, head_dim)
        .transpose(1, 0, 2)
        .reshape(row_count, full_width)
        .astype(jnp.bfloat16)
    )
    return ((key_part, value_part, gate_part), query_result)


def on_device(queries, key_vectors, values, forget_logit, out_grad, query_gain, key_gain, lengths):
    query_local = queries[0]
    key_local = key_vectors[0]
    value_local = values[0]
    logit_local = forget_logit[0]
    grad_local = out_grad[0]
    row_count, full_width = query_local.shape
    head_dim = key_local.shape[1]
    head_count = full_width // head_dim
    tile_dev = row_count // TILE
    servers = lax.axis_size("seq")
    owner_index = lax.axis_index("seq")
    tile_count = servers * tile_dev
    token_count = tile_count * TILE
    starts = tile_starts(lengths[0], tile_count)
    key_normed = norm_rows(key_local, key_gain, 1.0).astype(jnp.bfloat16)
    pads = prepare(
        (
            lax.all_gather(key_normed, "seq", axis=0, tiled=True),
            lax.all_gather(value_local, "seq", axis=0, tiled=True),
            lax.all_gather(logit_local, "seq", axis=1, tiled=True),
        )
    )
    lane_index = jnp.arange(tile_dev, dtype=jnp.int32)
    own_ids = owner_index * tile_dev + lane_index
    query_tiles = query_local.reshape(tile_dev, TILE, full_width)
    grad_tiles = grad_local.reshape(tile_dev, TILE, full_width)
    pad_set = pads
    out_tiles = lax.map(
        lambda task_item: forward_task(
            task_item[0],
            task_item[1],
            starts[task_item[1]],
            pad_set[0],
            pad_set[1],
            pad_set[2],
            query_gain,
            head_count,
        ),
        (query_tiles, own_ids),
    )
    pads = prepare(
        (
            lax.all_gather(key_normed, "seq", axis=0, tiled=True),
            lax.all_gather(value_local, "seq", axis=0, tiled=True),
            lax.all_gather(logit_local, "seq", axis=1, tiled=True),
        )
    )
    run_pad_set = pads
    zero_parts = (
        jnp.zeros(run_pad_set[0].shape, jnp.float32),
        jnp.zeros(run_pad_set[1].shape, jnp.float32),
        jnp.zeros(run_pad_set[2].shape, jnp.float32),
    )

    def task_step(partials, task_item):
        query_tile, grad_tile, out_tile, tile_id = task_item
        return backward_task(
            partials,
            query_tile,
            grad_tile,
            out_tile,
            tile_id,
            starts[tile_id],
            run_pad_set[0],
            run_pad_set[1],
            run_pad_set[2],
            query_gain,
            head_count,
        )

    partials, query_grad_tiles = lax.scan(
        task_step, zero_parts, (query_tiles, grad_tiles, out_tiles, own_ids)
    )
    key_part, value_part, gate_part = partials
    suffix = jnp.flip(jnp.cumsum(jnp.flip(gate_part[:, :token_count], 1), axis=1), 1)
    doc_most = tile_count * 3 // 4
    reach = min((doc_most + tile_dev - 2) // tile_dev, servers - 1)
    key_low = key_part[:token_count].astype(jnp.bfloat16)
    value_low = value_part[:token_count].astype(jnp.bfloat16)
    suffix_low = suffix.astype(jnp.bfloat16)

    def block_of(target):
        first_row = jnp.maximum(target, 0) * row_count
        return (
            lax.dynamic_slice_in_dim(key_low, first_row, row_count, 0),
            lax.dynamic_slice_in_dim(value_low, first_row, row_count, 0),
            lax.dynamic_slice_in_dim(suffix_low, first_row, row_count, 1),
        )

    own_block = block_of(owner_index)
    normed_key_grad = own_block[0].astype(jnp.float32)
    value_sum = own_block[1].astype(jnp.float32)
    gate_grad = own_block[2].astype(jnp.float32)
    for distance in range(1, reach + 1):
        piece = block_of(owner_index - distance)
        arrived_block = shifted((piece[0], piece[1], piece[2]), "seq", -distance)
        normed_key_grad = normed_key_grad + arrived_block[0].astype(jnp.float32)
        value_sum = value_sum + arrived_block[1].astype(jnp.float32)
        gate_grad = gate_grad + arrived_block[2].astype(jnp.float32)
    _, key_pullback = jax.vjp(
        lambda raw_values, gain_vec: norm_rows(raw_values, gain_vec, 1.0),
        key_local.astype(jnp.float32),
        key_gain,
    )
    key_input_grad, key_gain_part = key_pullback(normed_key_grad)
    scale_factor = head_dim ** (-0.5)
    _, query_pullback = jax.vjp(
        lambda raw_values, gain_vec: norm_rows(raw_values, gain_vec, scale_factor),
        query_local.reshape(row_count, head_count, head_dim).astype(jnp.float32),
        query_gain,
    )
    query_input_grad, query_gain_part = query_pullback(
        query_grad_tiles.reshape(row_count, head_count, head_dim).astype(jnp.float32)
    )
    forget_grad = gate_grad * jax.nn.sigmoid(-logit_local.astype(jnp.float32))
    gain_total = lax.psum(jnp.stack([query_gain_part, key_gain_part]), ("seq", "rep"))
    attention = out_tiles.reshape(row_count, full_width)
    return (
        attention[None],
        query_input_grad.reshape(row_count, full_width).astype(jnp.bfloat16)[None],
        key_input_grad.astype(jnp.bfloat16)[None],
        value_sum.astype(jnp.bfloat16)[None],
        forget_grad[None],
        gain_total,
    )


def solution(mesh):
    return jax.shard_map(
        on_device,
        mesh=mesh,
        in_specs=(
            P("rep", "seq", None),
            P("rep", "seq", None),
            P("rep", "seq", None),
            P("rep", None, "seq"),
            P("rep", "seq", None),
            P(),
            P(),
            P("rep", None),
        ),
        out_specs=(
            P("rep", "seq", None),
            P("rep", "seq", None),
            P("rep", "seq", None),
            P("rep", "seq", None),
            P("rep", None, "seq"),
            P(),
        ),
        check_vma=False,
    )
```

profile of v0, /device:TPU:12, one launch (start us, length us, event | category | flops | bytes accessed | tf_op | source)
XLA Modules:
  0.0 332.6 jit_solution(6965043462693032815)
XLA Ops:
  2.6 29.4 %all_gather.13 = bf16[2048,128]{1,0:T(8,128)(2,1)S(1)} all-gather(bf16[256,128]{1,0:T(8,128)(2,1)S(1)} %fusion.42), channel_id=1, replica_groups=mesh['seq'=8,'rep'=4] {'seq'}, dimensions={0}, use_global_device_ids=true | all-gather | bytes 589824 | tf_op jit(solution)/shard_map/all_gather | solution.py:253
  32.0 27.1 %all-gather = bf16[1,4,2048]{2,1,0:T(4,128)(2,1)S(1)} all-gather(bf16[1,4,256]{2,1,0:T(4,128)(2,1)} %param.21), channel_id=2, replica_groups=mesh['seq'=8,'rep'=4] {'seq'}, dimensions={2}, use_global_device_ids=true | all-gather | bytes 18432 | tf_op jit(solution)/shard_map/all_gather | solution.py:255
  60.8 28.6 %all-gather.1 = bf16[1,2048,128]{2,1,0:T(8,128)(2,1)S(1)} all-gather(bf16[1,256,128]{2,1,0:T(8,128)(2,1)} %param.20), channel_id=3, replica_groups=mesh['seq'=8,'rep'=4] {'seq'}, dimensions={1}, use_global_device_ids=true | all-gather | bytes 589824 | tf_op jit(solution)/shard_map/all_gather | solution.py:254
  90.5 33.2 %while.166 = (s32[]{:T(128)}, bf16[4,64,512]{2,1,0:T(8,128)(2,1)S(1)}, s32[4]{0:T(128)S(1)}, s32[32]{0:T(128)S(1)}, bf16[4,64,512]{2,1,0:T(8,128)(2,1)S(1)}, /*i...) while((s32[]{:T(128)}, ...), condition=%wide.region_10.11_spmd, body=%wide.region_5.10_spmd.sunk | while | flops 68126688 | bytes 5364638 | solution.py:263
  95.6 2.9 while.170
  104.0 2.9 while.170
  112.3 2.9 while.170
  120.6 2.9 while.170
  126.1 84.6 %while.169 = (s32[]{:T(128)}, f32[2560,128]{1,0:T(8,128)}, f32[2560,128]{1,0:T(8,128)}, f32[4,2560]{1,0:T(4,128)S(1)}, bf16[4,64,512]{2,1,0:T(8,128)(2,1)S(1)}, ...) while((s32[]{:T(128)}, f32[2560,128]{1,0:T(8,128)}, ...), condition=%wide.region_21.22_spmd, body=%wide.region_11.21_spmd.sunk | while | flops 204607008 | bytes 11740149 | solution.py:306
  131.3 2.3 while.171
  135.7 11.2 %while.172 = (s32[]{:T(128)}, f32[2560,128]{1,0:T(8,128)}, f32[2560,128]{1,0:T(8,128)}, f32[4,2560]{1,0:T(4,128)S(1)}, f32[256,128]{1,0:T(8,128)S(1)}, /*index=5...) while((s32[]{:T(128)}, f32[2560,128]{1,0:T(8,128)}, ...), condition=%wide.wide.region_20.20_spmd, body=%wide.wide.region_17.19_spmd.sunk | while | flops 170100288 | bytes 6100827 | solution.py:217
  136.6 2.0 fusion.133
  142.2 1.9 fusion.133
  152.4 2.3 while.171
  156.8 11.2 %while.172 = (s32[]{:T(128)}, f32[2560,128]{1,0:T(8,128)}, f32[2560,128]{1,0:T(8,128)}, f32[4,2560]{1,0:T(4,128)S(1)}, f32[256,128]{1,0:T(8,128)S(1)}, /*index=5...) while((s32[]{:T(128)}, f32[2560,128]{1,0:T(8,128)}, ...), condition=%wide.wide.region_20.20_spmd, body=%wide.wide.region_17.19_spmd.sunk | while | flops 170100288 | bytes 6100827 | solution.py:217
  157.7 2.0 fusion.133
  163.3 1.9 fusion.133
  173.6 2.3 while.171
  178.0 11.2 %while.172 = (s32[]{:T(128)}, f32[2560,128]{1,0:T(8,128)}, f32[2560,128]{1,0:T(8,128)}, f32[4,2560]{1,0:T(4,128)S(1)}, f32[256,128]{1,0:T(8,128)S(1)}, /*index=5...) while((s32[]{:T(128)}, f32[2560,128]{1,0:T(8,128)}, ...), condition=%wide.wide.region_20.20_spmd, body=%wide.wide.region_17.19_spmd.sunk | while | flops 170100288 | bytes 6100827 | solution.py:217
  178.9 2.0 fusion.133
  184.5 1.9 fusion.133
  194.7 2.3 while.171
  199.1 11.2 %while.172 = (s32[]{:T(128)}, f32[2560,128]{1,0:T(8,128)}, f32[2560,128]{1,0:T(8,128)}, f32[4,2560]{1,0:T(4,128)S(1)}, f32[256,128]{1,0:T(8,128)S(1)}, /*index=5...) while((s32[]{:T(128)}, f32[2560,128]{1,0:T(8,128)}, ...), condition=%wide.wide.region_20.20_spmd, body=%wide.wide.region_17.19_spmd.sunk | while | flops 170100288 | bytes 6100827 | solution.py:217
  200.0 2.0 fusion.133
  205.6 1.9 fusion.133
  230.7 8.8 %collective-permute-done.12 = bf16[4,256]{1,0:T(4,128)(2,1)S(1)} collective-permute-done((bf16[4,256]{1,0:T(4,128)(2,1)S(1)}, bf16[4,256]{1,0:T(4,128)(2,1)S(1)}, u32[]{:S(2)}, u32[]{:S(2)}) %collective-permute-start.12) | collective-permute-done | bytes 2080 | tf_op jit(solution)/shard_map/ppermute | solution.py:14
  240.1 19.3 %collective-permute-done.13 = bf16[4,256]{1,0:T(4,128)(2,1)S(1)} collective-permute-done((bf16[4,256]{1,0:T(4,128)(2,1)S(1)}, bf16[4,256]{1,0:T(4,128)(2,1)S(1)}, u32[]{:S(2)}, u32[]{:S(2)}) %collective-permute-start.13) | collective-permute-done | bytes 2080 | tf_op jit(solution)/shard_map/ppermute | solution.py:14
  260.1 2.0 collective-permute-done.14
  269.3 2.5 collective-permute-done.1
  276.6 4.1 %collective-permute-start.6 = (bf16[256,128]{1,0:T(8,128)(2,1)S(1)}, bf16[256,128]{1,0:T(8,128)(2,1)S(1)}, u32[]{:S(2)}, u32[]{:S(2)}) collective-permute-start(bf16[256,128]{1,0:T(8,128)(2,1)S(1)} %get-tuple-element.963), channel_id=1, source_target_pairs={{4,0},{8,4},{12,8},{16,12},{20,16},{24,20},{28,24},{5,1},{9,5},{13... | collective-permute-start | bytes 196616 | tf_op jit(solution)/shard_map/ppermute | solution.py:14
  280.7 3.2 collective-permute-start.7
  288.9 42.9 %psum.7 = f32[2,128]{1,0:T(2,128)} all-reduce(f32[2,128]{1,0:T(2,128)S(1)} %pad_maximum_fusion), channel_id=1, replica_groups=mesh['seq'=8,'rep'=4] {'seq','rep'}, use_global_device_ids=true, to_apply=%region_30.31 | all-reduce | flops 256 | bytes 2048 | tf_op jit(solution)/shard_map/psum | solution.py:351
  (633 shorter events, 119.1 us)
Async XLA Ops:
  0.6 88.8 %copy-start.9 = (s32[1,4]{1,0:T(1,128)S(1)}, s32[1,4]{1,0:T(1,128)}, u32[]{:S(2)}) copy-start(s32[1,4]{1,0:T(1,128)} %param.25) | copy-start | bytes 52
  136.6 3.9 %copy-start.2 = (f32[4,64]{1,0:T(4,128)S(1)}, f32[4,64]{1,0:T(4,128)}, u32[]{:S(2)}) copy-start(f32[4,64]{1,0:T(4,128)} %get-tuple-element.1761) | copy-start | bytes 3076 | tf_op jit(solution)/shard_map/while/body/eval_jaxpr/while
  142.2 3.9 %copy-start.2 = (f32[4,64]{1,0:T(4,128)S(1)}, f32[4,64]{1,0:T(4,128)}, u32[]{:S(2)}) copy-start(f32[4,64]{1,0:T(4,128)} %get-tuple-element.1761) | copy-start | bytes 3076 | tf_op jit(solution)/shard_map/while/body/eval_jaxpr/while
  157.7 3.9 %copy-start.2 = (f32[4,64]{1,0:T(4,128)S(1)}, f32[4,64]{1,0:T(4,128)}, u32[]{:S(2)}) copy-start(f32[4,64]{1,0:T(4,128)} %get-tuple-element.1761) | copy-start | bytes 3076 | tf_op jit(solution)/shard_map/while/body/eval_jaxpr/while
  163.3 3.9 %copy-start.2 = (f32[4,64]{1,0:T(4,128)S(1)}, f32[4,64]{1,0:T(4,128)}, u32[]{:S(2)}) copy-start(f32[4,64]{1,0:T(4,128)} %get-tuple-element.1761) | copy-start | bytes 3076 | tf_op jit(solution)/shard_map/while/body/eval_jaxpr/while
  178.9 3.9 %copy-start.2 = (f32[4,64]{1,0:T(4,128)S(1)}, f32[4,64]{1,0:T(4,128)}, u32[]{:S(2)}) copy-start(f32[4,64]{1,0:T(4,128)} %get-tuple-element.1761) | copy-start | bytes 3076 | tf_op jit(solution)/shard_map/while/body/eval_jaxpr/while
  184.5 3.9 %copy-start.2 = (f32[4,64]{1,0:T(4,128)S(1)}, f32[4,64]{1,0:T(4,128)}, u32[]{:S(2)}) copy-start(f32[4,64]{1,0:T(4,128)} %get-tuple-element.1761) | copy-start | bytes 3076 | tf_op jit(solution)/shard_map/while/body/eval_jaxpr/while
  200.0 3.9 %copy-start.2 = (f32[4,64]{1,0:T(4,128)S(1)}, f32[4,64]{1,0:T(4,128)}, u32[]{:S(2)}) copy-start(f32[4,64]{1,0:T(4,128)} %get-tuple-element.1761) | copy-start | bytes 3076 | tf_op jit(solution)/shard_map/while/body/eval_jaxpr/while
  205.6 3.9 %copy-start.2 = (f32[4,64]{1,0:T(4,128)S(1)}, f32[4,64]{1,0:T(4,128)}, u32[]{:S(2)}) copy-start(f32[4,64]{1,0:T(4,128)} %get-tuple-element.1761) | copy-start | bytes 3076 | tf_op jit(solution)/shard_map/while/body/eval_jaxpr/while
  210.8 15.1 %copy-start.4 = (bf16[4,64,512]{2,1,0:T(8,128)(2,1)}, bf16[4,64,512]{2,1,0:T(8,128)(2,1)S(1)}, u32[]{:S(2)}) copy-start(bf16[4,64,512]{2,1,0:T(8,128)(2,1)S(1)} %get-tuple-element.2002) | copy-start | bytes 786436
  212.2 13.6 %copy-start.3 = (bf16[2048,128]{1,0:T(8,128)(2,1)}, bf16[2048,128]{1,0:T(8,128)(2,1)S(1)}, u32[]{:S(2)}) copy-start(bf16[2048,128]{1,0:T(8,128)(2,1)S(1)} %slice.39) | copy-start | bytes 1572868
  212.2 55.8 %collective-permute-start = (bf16[256,128]{1,0:T(8,128)(2,1)S(1)}, bf16[256,128]{1,0:T(8,128)(2,1)S(1)}, u32[]{:S(2)}, u32[]{:S(2)}) collective-permute-start(bf16[256,128]{1,0:T(8,128)(2,1)S(1)} %get-tuple-element.969), channel_id=1, source_target_pairs={{4,0},{8,4},{12,8},{16,12},{20,16},{24,20},{28,24},{5,1},{9,5},{13... | collective-permute-start | bytes 196616 | tf_op jit(solution)/shard_map/ppermute | solution.py:14
  218.6 20.8 %collective-permute-start.12 = (bf16[4,256]{1,0:T(4,128)(2,1)S(1)}, bf16[4,256]{1,0:T(4,128)(2,1)S(1)}, u32[]{:S(2)}, u32[]{:S(2)}) collective-permute-start(bf16[4,256]{1,0:T(4,128)(2,1)S(1)} %get-tuple-element.975), channel_id=1, source_target_pairs={{4,0},{8,4},{12,8},{16,12},{20,16},{24,20},{28,24},{5,1},{9,5},{13... | collective-permute-start | bytes 6152 | tf_op jit(solution)/shard_map/ppermute | solution.py:14
  220.6 38.9 %collective-permute-start.13 = (bf16[4,256]{1,0:T(4,128)(2,1)S(1)}, bf16[4,256]{1,0:T(4,128)(2,1)S(1)}, u32[]{:S(2)}, u32[]{:S(2)}) collective-permute-start(bf16[4,256]{1,0:T(4,128)(2,1)S(1)} %get-tuple-element.979), channel_id=1, source_target_pairs={{8,0},{12,4},{16,8},{20,12},{24,16},{28,20},{9,1},{13,5},{17,9},{2... | collective-permute-start | bytes 6152 | tf_op jit(solution)/shard_map/ppermute | solution.py:14
  222.5 39.7 %collective-permute-start.14 = (bf16[4,256]{1,0:T(4,128)(2,1)S(1)}, bf16[4,256]{1,0:T(4,128)(2,1)S(1)}, u32[]{:S(2)}, u32[]{:S(2)}) collective-permute-start(bf16[4,256]{1,0:T(4,128)(2,1)S(1)} %get-tuple-element.978), channel_id=1, source_target_pairs={{12,0},{16,4},{20,8},{24,12},{28,16},{13,1},{17,5},{21,9},{25,13},... | collective-permute-start | bytes 6152 | tf_op jit(solution)/shard_map/ppermute | solution.py:14
  224.4 39.6 %collective-permute-start.15 = (bf16[4,256]{1,0:T(4,128)(2,1)S(1)}, bf16[4,256]{1,0:T(4,128)(2,1)S(1)}, u32[]{:S(2)}, u32[]{:S(2)}) collective-permute-start(bf16[4,256]{1,0:T(4,128)(2,1)S(1)} %get-tuple-element.977), channel_id=1, source_target_pairs={{16,0},{20,4},{24,8},{28,12},{17,1},{21,5},{25,9},{29,13},{18,2},{... | collective-permute-start | bytes 6152 | tf_op jit(solution)/shard_map/ppermute | solution.py:14
  229.3 39.4 %copy-start.7 = (bf16[1,4,256]{2,1,0:T(4,128)(2,1)S(1)}, bf16[1,4,256]{2,1,0:T(4,128)(2,1)}, u32[]{:S(2)}) copy-start(bf16[1,4,256]{2,1,0:T(4,128)(2,1)} %param.21) | copy-start | bytes 6148
  229.3 56.5 %copy-start.5 = (bf16[1,256,128]{2,1,0:T(8,128)(2,1)S(1)}, bf16[1,256,128]{2,1,0:T(8,128)(2,1)}, u32[]{:S(2)}) copy-start(bf16[1,256,128]{2,1,0:T(8,128)(2,1)} %param.19) | copy-start | bytes 196612
  229.3 56.5 %copy-start.8 = (f32[128]{0:T(128)S(1)}, f32[128]{0:T(128)}, u32[]{:S(2)}) copy-start(f32[128]{0:T(128)} %param.24) | copy-start | bytes 1540
  239.5 26.5 %collective-permute-start.16 = (bf16[4,256]{1,0:T(4,128)(2,1)S(1)}, bf16[4,256]{1,0:T(4,128)(2,1)S(1)}, u32[]{:S(2)}, u32[]{:S(2)}) collective-permute-start(bf16[4,256]{1,0:T(4,128)(2,1)S(1)} %get-tuple-element.976), channel_id=1, source_target_pairs={{20,0},{24,4},{28,8},{21,1},{25,5},{29,9},{22,2},{26,6},{30,10},{2... | collective-permute-start | bytes 6152 | tf_op jit(solution)/shard_map/ppermute | solution.py:14
  259.4 7.9 %collective-permute-start.17 = (bf16[4,256]{1,0:T(4,128)(2,1)S(1)}, bf16[4,256]{1,0:T(4,128)(2,1)S(1)}, u32[]{:S(2)}, u32[]{:S(2)}) collective-permute-start(bf16[4,256]{1,0:T(4,128)(2,1)S(1)} %get-tuple-element.980), channel_id=1, source_target_pairs={{24,0},{28,4},{25,1},{29,5},{26,2},{30,6},{27,3},{31,7}} | collective-permute-start | bytes 6152 | tf_op jit(solution)/shard_map/ppermute | solution.py:14
  262.1 9.6 %collective-permute-start.1 = (bf16[256,128]{1,0:T(8,128)(2,1)S(1)}, bf16[256,128]{1,0:T(8,128)(2,1)S(1)}, u32[]{:S(2)}, u32[]{:S(2)}) collective-permute-start(bf16[256,128]{1,0:T(8,128)(2,1)S(1)} %get-tuple-element.973), channel_id=1, source_target_pairs={{8,0},{12,4},{16,8},{20,12},{24,16},{28,20},{9,1},{13,5},{17,9},{2... | collective-permute-start | bytes 196616 | tf_op jit(solution)/shard_map/ppermute | solution.py:14
  264.1 10.3 %collective-permute-start.2 = (bf16[256,128]{1,0:T(8,128)(2,1)S(1)}, bf16[256,128]{1,0:T(8,128)(2,1)S(1)}, u32[]{:S(2)}, u32[]{:S(2)}) collective-permute-start(bf16[256,128]{1,0:T(8,128)(2,1)S(1)} %get-tuple-element.972), channel_id=1, source_target_pairs={{12,0},{16,4},{20,8},{24,12},{28,16},{13,1},{17,5},{21,9},{25,13},... | collective-permute-start | bytes 196616 | tf_op jit(solution)/shard_map/ppermute | solution.py:14
  266.0 10.6 %collective-permute-start.3 = (bf16[256,128]{1,0:T(8,128)(2,1)S(1)}, bf16[256,128]{1,0:T(8,128)(2,1)S(1)}, u32[]{:S(2)}, u32[]{:S(2)}) collective-permute-start(bf16[256,128]{1,0:T(8,128)(2,1)S(1)} %get-tuple-element.971), channel_id=1, source_target_pairs={{16,0},{20,4},{24,8},{28,12},{17,1},{21,5},{25,9},{29,13},{18,2},{... | collective-permute-start | bytes 196616 | tf_op jit(solution)/shard_map/ppermute | solution.py:14
  267.3 13.3 %collective-permute-start.4 = (bf16[256,128]{1,0:T(8,128)(2,1)S(1)}, bf16[256,128]{1,0:T(8,128)(2,1)S(1)}, u32[]{:S(2)}, u32[]{:S(2)}) collective-permute-start(bf16[256,128]{1,0:T(8,128)(2,1)S(1)} %get-tuple-element.970), channel_id=1, source_target_pairs={{20,0},{24,4},{28,8},{21,1},{25,5},{29,9},{22,2},{26,6},{30,10},{2... | collective-permute-start | bytes 196616 | tf_op jit(solution)/shard_map/ppermute | solution.py:14
  268.0 15.8 %collective-permute-start.5 = (bf16[256,128]{1,0:T(8,128)(2,1)S(1)}, bf16[256,128]{1,0:T(8,128)(2,1)S(1)}, u32[]{:S(2)}, u32[]{:S(2)}) collective-permute-start(bf16[256,128]{1,0:T(8,128)(2,1)S(1)} %get-tuple-element.974), channel_id=1, source_target_pairs={{24,0},{28,4},{25,1},{29,5},{26,2},{30,6},{27,3},{31,7}} | collective-permute-start | bytes 196616 | tf_op jit(solution)/shard_map/ppermute | solution.py:14
  271.8 15.8 %collective-permute-start.10 = (bf16[256,128]{1,0:T(8,128)(2,1)S(1)}, bf16[256,128]{1,0:T(8,128)(2,1)S(1)}, u32[]{:S(2)}, u32[]{:S(2)}) collective-permute-start(bf16[256,128]{1,0:T(8,128)(2,1)S(1)} %get-tuple-element.964), channel_id=1, source_target_pairs={{20,0},{24,4},{28,8},{21,1},{25,5},{29,9},{22,2},{26,6},{30,10},{2... | collective-permute-start | bytes 196616 | tf_op jit(solution)/shard_map/ppermute | solution.py:14
  274.4 57.5 %collective-permute-start.11 = (bf16[256,128]{1,0:T(8,128)(2,1)S(1)}, bf16[256,128]{1,0:T(8,128)(2,1)S(1)}, u32[]{:S(2)}, u32[]{:S(2)}) collective-permute-start(bf16[256,128]{1,0:T(8,128)(2,1)S(1)} %get-tuple-element.968), channel_id=1, source_target_pairs={{24,0},{28,4},{25,1},{29,5},{26,2},{30,6},{27,3},{31,7}} | collective-permute-start | bytes 196616 | tf_op jit(solution)/shard_map/ppermute | solution.py:14
  276.6 55.3 %collective-permute-start.6 = (bf16[256,128]{1,0:T(8,128)(2,1)S(1)}, bf16[256,128]{1,0:T(8,128)(2,1)S(1)}, u32[]{:S(2)}, u32[]{:S(2)}) collective-permute-start(bf16[256,128]{1,0:T(8,128)(2,1)S(1)} %get-tuple-element.963), channel_id=1, source_target_pairs={{4,0},{8,4},{12,8},{16,12},{20,16},{24,20},{28,24},{5,1},{9,5},{13... | collective-permute-start | bytes 196616 | tf_op jit(solution)/shard_map/ppermute | solution.py:14
  280.7 51.2 %collective-permute-start.7 = (bf16[256,128]{1,0:T(8,128)(2,1)S(1)}, bf16[256,128]{1,0:T(8,128)(2,1)S(1)}, u32[]{:S(2)}, u32[]{:S(2)}) collective-permute-start(bf16[256,128]{1,0:T(8,128)(2,1)S(1)} %get-tuple-element.967), channel_id=1, source_target_pairs={{8,0},{12,4},{16,8},{20,12},{24,16},{28,20},{9,1},{13,5},{17,9},{2... | collective-permute-start | bytes 196616 | tf_op jit(solution)/shard_map/ppermute | solution.py:14
  283.8 48.0 %collective-permute-start.8 = (bf16[256,128]{1,0:T(8,128)(2,1)S(1)}, bf16[256,128]{1,0:T(8,128)(2,1)S(1)}, u32[]{:S(2)}, u32[]{:S(2)}) collective-permute-start(bf16[256,128]{1,0:T(8,128)(2,1)S(1)} %get-tuple-element.966), channel_id=1, source_target_pairs={{12,0},{16,4},{20,8},{24,12},{28,16},{13,1},{17,5},{21,9},{25,13},... | collective-permute-start | bytes 196616 | tf_op jit(solution)/shard_map/ppermute | solution.py:14
  287.6 44.3 %collective-permute-start.9 = (bf16[256,128]{1,0:T(8,128)(2,1)S(1)}, bf16[256,128]{1,0:T(8,128)(2,1)S(1)}, u32[]{:S(2)}, u32[]{:S(2)}) collective-permute-start(bf16[256,128]{1,0:T(8,128)(2,1)S(1)} %get-tuple-element.965), channel_id=1, source_target_pairs={{16,0},{20,4},{24,8},{28,12},{17,1},{21,5},{25,9},{29,13},{18,2},{... | collective-permute-start | bytes 196616 | tf_op jit(solution)/shard_map/ppermute | solution.py:14
  (10 other events, 6.5 us)
where the time goes:
time: 335 us; the launch traced here: 333 us
  blocking collectives  128 us (38%)
  local copies, waits for them, and re-layouts  45.9 us (14%)
  matrix products  44.9 us (13%)
  waiting for transfers between devices  36.1 us (11%)
  loops' own time  28.8 us (9%)
  starting transfers between devices  28.5 us (9%)
  other arithmetic  19.3 us (6%)
    psum x1, blocking collectives, on_device(): lax.psum(jnp.stack([query_gain_part, key_gain_part]), ('seq', 'rep'))  42.9 us
    ppermute x18, waiting for transfers between devices, shifted(): lax.ppermute(value, axis, [(source, source + steps) for source in range(i...  36.1 us
    dot_general x16, matrix products, contract_first(): lax.dot_general(left_rows, right_rows, (((0,), (0,)), ((), ())), preferre...  30.9 us
    all_gather x1, blocking collectives, on_device(): lax.all_gather(key_normed, 'seq', axis=0, tiled=True)  29.4 us
    all_gather x1, blocking collectives, on_device(): lax.all_gather(value_local, 'seq', axis=0, tiled=True)  28.6 us
    ppermute x18, starting transfers between devices, shifted(): lax.ppermute(value, axis, [(source, source + steps) for source in range(i...  28.5 us
    all_gather x1, blocking collectives, on_device(): lax.all_gather(logit_local, 'seq', axis=1, tiled=True)  27.1 us
    another operation x1, loops' own time, on_device(): lax.scan(task_step, zero_parts, (query_tiles, grad_tiles, out_tiles, own_...  13.7 us
  transfers between devices with their start and end apart: 18, of which 6 were waited for; matrix products, arithmetic and copies ran while one was open for 4% of the time, Pallas kernels for 0%

commit v1 on v0

--- a/solution.py
+++ b/solution.py
@@ -6,6 +6,18 @@
 TILE = 64
 norm_eps = 1e-06
 key_span = 512
+
+
+def collect(array, axis, dim):
+    ways, here = (lax.axis_size(axis), lax.axis_index(axis))
+    grown, reach = (array, 1)
+    while reach < ways:
+        theirs = lax.ppermute(grown, axis, [(d, d ^ reach) for d in range(ways)])
+        mine_first = jnp.concatenate([grown, theirs], axis=dim)
+        theirs_first = jnp.concatenate([theirs, grown], axis=dim)
+        grown = jnp.where(here & reach == 0, mine_first, theirs_first)
+        reach = 2 * reach
+    return grown
 
 
 def shifted(value, axis, steps):
@@ -250,7 +262,7 @@
     key_normed = norm_rows(key_local, key_gain, 1.0).astype(jnp.bfloat16)
     pads = prepare(
         (
-            lax.all_gather(key_normed, "seq", axis=0, tiled=True),
+            collect(key_normed, "seq", 0),
             lax.all_gather(value_local, "seq", axis=0, tiled=True),
             lax.all_gather(logit_local, "seq", axis=1, tiled=True),
         )

time: 335 us -> 357 us (1.066)
  starting transfers between devices: 28.5 us -> 36.2 us
  blocking collectives: 128 us -> 133 us
  local copies, waits for them, and re-layouts: 45.9 us -> 49.6 us
    ppermute x0 -> x3, starting transfers between devices: none -> 7.7 us  [collect(): theirs = lax.ppermute(grown, axis, [(d, d ^ reach) for d in range(ways)])]
    ppermute x0 -> x3, waiting for transfers between devices: none -> 7.08 us  [collect(): theirs = lax.ppermute(grown, axis, [(d, d ^ reach) for d in range(ways)])]
    psum x1, blocking collectives: 42.9 us -> 47.9 us  [on_device(): lax.psum(jnp.stack([query_gain_part, key_gain_part]), ('seq', 'rep'))]
    ppermute x18, waiting for transfers between devices: 36.1 us -> 32 us  [shifted(): lax.ppermute(value, axis, [(source, source + steps) for source in range(i...]
  transfers between devices with their start and end apart: 18 -> 21, of which waited for: 6 -> 5; matrix products, arithmetic and copies ran while one was open for 4% -> 4% of each run, Pallas kernels for 0% -> 0%
where the time goes in v1:
time: 357 us; the launch traced here: 355 us
  blocking collectives  133 us (37%)
  local copies, waits for them, and re-layouts  49.6 us (14%)
  matrix products  44.9 us (13%)
  waiting for transfers between devices  39.1 us (11%)
  starting transfers between devices  36.2 us (10%)
  loops' own time  28.7 us (8%)
  other arithmetic  22.1 us (6%)
    psum x1, blocking collectives, on_device(): lax.psum(jnp.stack([query_gain_part, key_gain_part]), ('seq', 'rep'))  47.9 us
    ppermute x18, waiting for transfers between devices, shifted(): lax.ppermute(value, axis, [(source, source + steps) for source in range(i...  32 us
    dot_general x16, matrix products, contract_first(): lax.dot_general(left_rows, right_rows, (((0,), (0,)), ((), ())), preferre...  30.9 us
    all_gather x1, blocking collectives, on_device(): lax.all_gather(key_normed, 'seq', axis=0, tiled=True)  29.2 us
    all_gather x1, blocking collectives, on_device(): lax.all_gather(value_local, 'seq', axis=0, tiled=True)  28.8 us
    ppermute x18, starting transfers between devices, shifted(): lax.ppermute(value, axis, [(source, source + steps) for source in range(i...  28.5 us
    all_gather x1, blocking collectives, on_device(): lax.all_gather(logit_local, 'seq', axis=1, tiled=True)  27.6 us
    another operation x1, loops' own time, on_device(): lax.scan(task_step, zero_parts, (query_tiles, grad_tiles, out_tiles, own_...  13.7 us
  transfers between devices with their start and end apart: 21, of which 5 were waited for; matrix products, arithmetic and copies ran while one was open for 4% of the time, Pallas kernels for 0%

profile of v1, /device:TPU:12, one launch (start us, length us, event | category | flops | bytes accessed | tf_op | source)
XLA Modules:
  0.0 355.2 jit_solution(14973590054439431008)
XLA Ops:
  3.2 29.2 %all_gather.13 = bf16[2048,128]{1,0:T(8,128)(2,1)S(1)} all-gather(bf16[256,128]{1,0:T(8,128)(2,1)S(1)} %fusion.42), channel_id=1, replica_groups=mesh['seq'=8,'rep'=4] {'seq'}, dimensions={0}, use_global_device_ids=true | all-gather | bytes 589824 | tf_op jit(solution)/shard_map/all_gather | solution.py:290
  32.4 27.6 %all-gather = bf16[1,4,2048]{2,1,0:T(4,128)(2,1)S(1)} all-gather(bf16[1,4,256]{2,1,0:T(4,128)(2,1)} %param.21), channel_id=2, replica_groups=mesh['seq'=8,'rep'=4] {'seq'}, dimensions={2}, use_global_device_ids=true | all-gather | bytes 18432 | tf_op jit(solution)/shard_map/all_gather | solution.py:267
  61.4 28.8 %all-gather.1 = bf16[1,2048,128]{2,1,0:T(8,128)(2,1)S(1)} all-gather(bf16[1,256,128]{2,1,0:T(8,128)(2,1)} %param.20), channel_id=3, replica_groups=mesh['seq'=8,'rep'=4] {'seq'}, dimensions={1}, use_global_device_ids=true | all-gather | bytes 589824 | tf_op jit(solution)/shard_map/all_gather | solution.py:266
  90.5 3.7 %collective-permute-start.1 = (bf16[512,128]{1,0:T(8,128)(2,1)S(1)}, bf16[512,128]{1,0:T(8,128)(2,1)S(1)}, u32[]{:S(2)}, u32[]{:S(2)}) collective-permute-start(bf16[512,128]{1,0:T(8,128)(2,1)S(1)} %maximum_select_fusion.2), channel_id=1, source_target_pairs={{0,8},{4,12},{8,0},{12,4},{16,24},{20,28},{24,16},{28,20},{1,9},{5... | collective-permute-start | bytes 393224 | tf_op jit(solution)/shard_map/ppermute | solution.py:15
  94.4 2.7 collective-permute-done.1
  97.2 3.5 collective-permute-start.2
  102.4 4.4 %collective-permute-done.2 = bf16[1024,128]{1,0:T(8,128)(2,1)S(1)} collective-permute-done((bf16[1024,128]{1,0:T(8,128)(2,1)S(1)}, bf16[1024,128]{1,0:T(8,128)(2,1)S(1)}, u32[]{:S(2)}, u32[]{:S(2)}) %collective-permute-start.2) | collective-permute-done | bytes 262176 | tf_op jit(solution)/shard_map/ppermute | solution.py:15
  107.7 35.6 %while.166 = (s32[]{:T(128)}, bf16[4,64,512]{2,1,0:T(8,128)(2,1)}, s32[4]{0:T(128)S(1)}, s32[32]{0:T(128)S(1)}, bf16[4,64,512]{2,1,0:T(8,128)(2,1)S(1)}, /*index...) while((s32[]{:T(128)}, bf16[4,64,512]{2,1,0:T(8,128)(2,1)}, ...), condition=%wide.region_10.11_spmd, body=%wide.region_5.10_spmd.sunk | while | flops 68126688 | bytes 5365146 | solution.py:275
  112.8 2.9 while.170
  121.7 2.9 while.170
  130.6 2.9 while.170
  139.5 2.9 while.170
  145.7 87.9 %while.169 = (s32[]{:T(128)}, f32[2560,128]{1,0:T(8,128)}, f32[2560,128]{1,0:T(8,128)}, f32[4,2560]{1,0:T(4,128)S(1)}, bf16[4,64,512]{2,1,0:T(8,128)(2,1)S(1)}, ...) while((s32[]{:T(128)}, f32[2560,128]{1,0:T(8,128)}, ...), condition=%wide.region_21.22_spmd, body=%wide.region_11.21_spmd.sunk | while | flops 204607008 | bytes 11740149 | solution.py:318
  151.6 2.3 while.171
  156.1 11.2 %while.172 = (s32[]{:T(128)}, f32[2560,128]{1,0:T(8,128)}, f32[2560,128]{1,0:T(8,128)}, f32[4,2560]{1,0:T(4,128)S(1)}, f32[256,128]{1,0:T(8,128)S(1)}, /*index=5...) while((s32[]{:T(128)}, f32[2560,128]{1,0:T(8,128)}, ...), condition=%wide.wide.region_20.20_spmd, body=%wide.wide.region_17.19_spmd.sunk | while | flops 170100288 | bytes 6100827 | solution.py:229
  156.9 2.0 fusion.133
  162.5 1.9 fusion.133
  173.5 2.3 while.171
  178.0 11.2 %while.172 = (s32[]{:T(128)}, f32[2560,128]{1,0:T(8,128)}, f32[2560,128]{1,0:T(8,128)}, f32[4,2560]{1,0:T(4,128)S(1)}, f32[256,128]{1,0:T(8,128)S(1)}, /*index=5...) while((s32[]{:T(128)}, f32[2560,128]{1,0:T(8,128)}, ...), condition=%wide.wide.region_20.20_spmd, body=%wide.wide.region_17.19_spmd.sunk | while | flops 170100288 | bytes 6100827 | solution.py:229
  178.9 2.0 fusion.133
  195.5 2.3 while.171
  200.0 11.2 %while.172 = (s32[]{:T(128)}, f32[2560,128]{1,0:T(8,128)}, f32[2560,128]{1,0:T(8,128)}, f32[4,2560]{1,0:T(4,128)S(1)}, f32[256,128]{1,0:T(8,128)S(1)}, /*index=5...) while((s32[]{:T(128)}, f32[2560,128]{1,0:T(8,128)}, ...), condition=%wide.wide.region_20.20_spmd, body=%wide.wide.region_17.19_spmd.sunk | while | flops 170100288 | bytes 6100827 | solution.py:229
  200.9 2.0 fusion.133
  217.5 2.3 while.171
  222.0 11.2 %while.172 = (s32[]{:T(128)}, f32[2560,128]{1,0:T(8,128)}, f32[2560,128]{1,0:T(8,128)}, f32[4,2560]{1,0:T(4,128)S(1)}, f32[256,128]{1,0:T(8,128)S(1)}, /*index=5...) while((s32[]{:T(128)}, f32[2560,128]{1,0:T(8,128)}, ...), condition=%wide.wide.region_20.20_spmd, body=%wide.wide.region_17.19_spmd.sunk | while | flops 170100288 | bytes 6100827 | solution.py:229
  222.8 2.0 fusion.133
  253.3 14.0 %collective-permute-done.15 = bf16[4,256]{1,0:T(4,128)(2,1)S(1)} collective-permute-done((bf16[4,256]{1,0:T(4,128)(2,1)S(1)}, bf16[4,256]{1,0:T(4,128)(2,1)S(1)}, u32[]{:S(2)}, u32[]{:S(2)}) %collective-permute-start.15) | collective-permute-done | bytes 2080 | tf_op jit(solution)/shard_map/ppermute | solution.py:26
  267.9 15.9 %collective-permute-done.16 = bf16[4,256]{1,0:T(4,128)(2,1)S(1)} collective-permute-done((bf16[4,256]{1,0:T(4,128)(2,1)S(1)}, bf16[4,256]{1,0:T(4,128)(2,1)S(1)}, u32[]{:S(2)}, u32[]{:S(2)}) %collective-permute-start.16) | collective-permute-done | bytes 2080 | tf_op jit(solution)/shard_map/ppermute | solution.py:26
  284.5 2.1 collective-permute-done.17
  293.8 5.2 %collective-permute-start.10 = (bf16[256,128]{1,0:T(8,128)(2,1)S(1)}, bf16[256,128]{1,0:T(8,128)(2,1)S(1)}, u32[]{:S(2)}, u32[]{:S(2)}) collective-permute-start(bf16[256,128]{1,0:T(8,128)(2,1)S(1)} %get-tuple-element.967), channel_id=1, source_target_pairs={{8,0},{12,4},{16,8},{20,12},{24,16},{28,20},{9,1},{13,5},{17,9},{2... | collective-permute-start | bytes 196616 | tf_op jit(solution)/shard_map/ppermute | solution.py:26
  304.6 2.0 collective-permute-start.9
  306.7 47.9 %psum.7 = f32[2,128]{1,0:T(2,128)} all-reduce(f32[2,128]{1,0:T(2,128)S(1)} %pad_maximum_fusion), channel_id=1, replica_groups=mesh['seq'=8,'rep'=4] {'seq','rep'}, use_global_device_ids=true, to_apply=%region_30.31 | all-reduce | flops 256 | bytes 2048 | tf_op jit(solution)/shard_map/psum | solution.py:363
  (655 shorter events, 128.7 us)
Async XLA Ops:
  0.6 93.5 %copy-start.16 = (f32[128]{0:T(128)S(1)}, f32[128]{0:T(128)}, u32[]{:S(2)}) copy-start(f32[128]{0:T(128)} %param.23) | copy-start | bytes 1540
  0.6 93.5 %copy-start.15 = (s32[1,4]{1,0:T(1,128)S(1)}, s32[1,4]{1,0:T(1,128)}, u32[]{:S(2)}) copy-start(s32[1,4]{1,0:T(1,128)} %param.25) | copy-start | bytes 52
  0.7 100.0 %copy-start = (bf16[1,256,512]{2,1,0:T(8,128)(2,1)S(1)}, bf16[1,256,512]{2,1,0:T(8,128)(2,1)}, u32[]{:S(2)}) copy-start(bf16[1,256,512]{2,1,0:T(8,128)(2,1)} %param.18) | copy-start | bytes 786436
  1.7 30.7 %copy-start.8 = (f32[256]{0:T(256)}, f32[256]{0:T(256)S(1)}, u32[]{:S(2)}) copy-start(f32[256]{0:T(256)S(1)} %fusion.45) | copy-start | bytes 3076
  1.7 30.7 %copy-start.6 = (f32[256]{0:T(256)}, f32[256]{0:T(256)S(1)}, u32[]{:S(2)}) copy-start(f32[256]{0:T(256)S(1)} %fusion.57) | copy-start | bytes 3076
  2.6 87.8 %collective-permute-start = (bf16[256,128]{1,0:T(8,128)(2,1)S(1)}, bf16[256,128]{1,0:T(8,128)(2,1)S(1)}, u32[]{:S(2)}, u32[]{:S(2)}) collective-permute-start(bf16[256,128]{1,0:T(8,128)(2,1)S(1)} %fusion.42), channel_id=1, source_target_pairs={{0,4},{4,0},{8,12},{12,8},{16,20},{20,16},{24,28},{28,24},{1,5},{5... | collective-permute-start | bytes 196616 | tf_op jit(solution)/shard_map/ppermute | solution.py:15
  90.5 6.6 %collective-permute-start.1 = (bf16[512,128]{1,0:T(8,128)(2,1)S(1)}, bf16[512,128]{1,0:T(8,128)(2,1)S(1)}, u32[]{:S(2)}, u32[]{:S(2)}) collective-permute-start(bf16[512,128]{1,0:T(8,128)(2,1)S(1)} %maximum_select_fusion.2), channel_id=1, source_target_pairs={{0,8},{4,12},{8,0},{12,4},{16,24},{20,28},{24,16},{28,20},{1,9},{5... | collective-permute-start | bytes 393224 | tf_op jit(solution)/shard_map/ppermute | solution.py:15
  94.2 7.6 %copy-start.13 = (f32[128]{0:T(128)}, f32[128]{0:T(128)S(1)}, u32[]{:S(2)}) copy-start(f32[128]{0:T(128)S(1)} %broadcast_multiply_fusion.2) | copy-start | bytes 1540
  97.2 9.6 %collective-permute-start.2 = (bf16[1024,128]{1,0:T(8,128)(2,1)S(1)}, bf16[1024,128]{1,0:T(8,128)(2,1)S(1)}, u32[]{:S(2)}, u32[]{:S(2)}) collective-permute-start(bf16[1024,128]{1,0:T(8,128)(2,1)S(1)} %maximum_select_fusion.1), channel_id=1, source_target_pairs={{0,16},{4,20},{8,24},{12,28},{16,0},{20,4},{24,8},{28,12},{1,17},{... | collective-permute-start | bytes 786440 | tf_op jit(solution)/shard_map/ppermute | solution.py:15
  235.2 57.2 %collective-permute-start.3 = (bf16[256,128]{1,0:T(8,128)(2,1)S(1)}, bf16[256,128]{1,0:T(8,128)(2,1)S(1)}, u32[]{:S(2)}, u32[]{:S(2)}) collective-permute-start(bf16[256,128]{1,0:T(8,128)(2,1)S(1)} %get-tuple-element.969), channel_id=1, source_target_pairs={{4,0},{8,4},{12,8},{16,12},{20,16},{24,20},{28,24},{5,1},{9,5},{13... | collective-permute-start | bytes 196616 | tf_op jit(solution)/shard_map/ppermute | solution.py:26
  240.3 52.8 %copy-start.10 = (bf16[1,4,256]{2,1,0:T(4,128)(2,1)S(1)}, bf16[1,4,256]{2,1,0:T(4,128)(2,1)}, u32[]{:S(2)}) copy-start(bf16[1,4,256]{2,1,0:T(4,128)(2,1)} %param.21) | copy-start | bytes 6148
  240.3 63.2 %copy-start.4 = (bf16[1,256,128]{2,1,0:T(8,128)(2,1)S(1)}, bf16[1,256,128]{2,1,0:T(8,128)(2,1)}, u32[]{:S(2)}) copy-start(bf16[1,256,128]{2,1,0:T(8,128)(2,1)} %param.19) | copy-start | bytes 196612
  240.3 63.3 %copy-start.7 = (f32[256]{0:T(256)S(1)}, f32[256]{0:T(256)}, u32[]{:S(2)}) copy-start(f32[256]{0:T(256)} %copy-done.6) | copy-start | bytes 3076
  240.3 63.3 %copy-start.12 = (f32[128]{0:T(128)S(1)}, f32[128]{0:T(128)}, u32[]{:S(2)}) copy-start(f32[128]{0:T(128)} %param.24) | copy-start | bytes 1540
  243.4 60.4 %copy-start.9 = (f32[256]{0:T(256)S(1)}, f32[256]{0:T(256)}, u32[]{:S(2)}) copy-start(f32[256]{0:T(256)} %copy-done.8) | copy-start | bytes 3076
  244.9 22.4 %collective-permute-start.15 = (bf16[4,256]{1,0:T(4,128)(2,1)S(1)}, bf16[4,256]{1,0:T(4,128)(2,1)S(1)}, u32[]{:S(2)}, u32[]{:S(2)}) collective-permute-start(bf16[4,256]{1,0:T(4,128)(2,1)S(1)} %get-tuple-element.975), channel_id=1, source_target_pairs={{4,0},{8,4},{12,8},{16,12},{20,16},{24,20},{28,24},{5,1},{9,5},{13... | collective-permute-start | bytes 6152 | tf_op jit(solution)/shard_map/ppermute | solution.py:26
  246.8 37.0 %collective-permute-start.16 = (bf16[4,256]{1,0:T(4,128)(2,1)S(1)}, bf16[4,256]{1,0:T(4,128)(2,1)S(1)}, u32[]{:S(2)}, u32[]{:S(2)}) collective-permute-start(bf16[4,256]{1,0:T(4,128)(2,1)S(1)} %get-tuple-element.979), channel_id=1, source_target_pairs={{8,0},{12,4},{16,8},{20,12},{24,16},{28,20},{9,1},{13,5},{17,9},{2... | collective-permute-start | bytes 6152 | tf_op jit(solution)/shard_map/ppermute | solution.py:26
  248.7 37.9 %collective-permute-start.17 = (bf16[4,256]{1,0:T(4,128)(2,1)S(1)}, bf16[4,256]{1,0:T(4,128)(2,1)S(1)}, u32[]{:S(2)}, u32[]{:S(2)}) collective-permute-start(bf16[4,256]{1,0:T(4,128)(2,1)S(1)} %get-tuple-element.978), channel_id=1, source_target_pairs={{12,0},{16,4},{20,8},{24,12},{28,16},{13,1},{17,5},{21,9},{25,13},... | collective-permute-start | bytes 6152 | tf_op jit(solution)/shard_map/ppermute | solution.py:26
  250.7 37.9 %collective-permute-start.18 = (bf16[4,256]{1,0:T(4,128)(2,1)S(1)}, bf16[4,256]{1,0:T(4,128)(2,1)S(1)}, u32[]{:S(2)}, u32[]{:S(2)}) collective-permute-start(bf16[4,256]{1,0:T(4,128)(2,1)S(1)} %get-tuple-element.977), channel_id=1, source_target_pairs={{16,0},{20,4},{24,8},{28,12},{17,1},{21,5},{25,9},{29,13},{18,2},{... | collective-permute-start | bytes 6152 | tf_op jit(solution)/shard_map/ppermute | solution.py:26
  267.2 23.2 %collective-permute-start.19 = (bf16[4,256]{1,0:T(4,128)(2,1)S(1)}, bf16[4,256]{1,0:T(4,128)(2,1)S(1)}, u32[]{:S(2)}, u32[]{:S(2)}) collective-permute-start(bf16[4,256]{1,0:T(4,128)(2,1)S(1)} %get-tuple-element.976), channel_id=1, source_target_pairs={{20,0},{24,4},{28,8},{21,1},{25,5},{29,9},{22,2},{26,6},{30,10},{2... | collective-permute-start | bytes 6152 | tf_op jit(solution)/shard_map/ppermute | solution.py:26
  283.8 8.0 %collective-permute-start.20 = (bf16[4,256]{1,0:T(4,128)(2,1)S(1)}, bf16[4,256]{1,0:T(4,128)(2,1)S(1)}, u32[]{:S(2)}, u32[]{:S(2)}) collective-permute-start(bf16[4,256]{1,0:T(4,128)(2,1)S(1)} %get-tuple-element.980), channel_id=1, source_target_pairs={{24,0},{28,4},{25,1},{29,5},{26,2},{30,6},{27,3},{31,7}} | collective-permute-start | bytes 6152 | tf_op jit(solution)/shard_map/ppermute | solution.py:26
  286.6 7.2 %collective-permute-start.4 = (bf16[256,128]{1,0:T(8,128)(2,1)S(1)}, bf16[256,128]{1,0:T(8,128)(2,1)S(1)}, u32[]{:S(2)}, u32[]{:S(2)}) collective-permute-start(bf16[256,128]{1,0:T(8,128)(2,1)S(1)} %get-tuple-element.973), channel_id=1, source_target_pairs={{8,0},{12,4},{16,8},{20,12},{24,16},{28,20},{9,1},{13,5},{17,9},{2... | collective-permute-start | bytes 196616 | tf_op jit(solution)/shard_map/ppermute | solution.py:26
  288.5 10.4 %collective-permute-start.5 = (bf16[256,128]{1,0:T(8,128)(2,1)S(1)}, bf16[256,128]{1,0:T(8,128)(2,1)S(1)}, u32[]{:S(2)}, u32[]{:S(2)}) collective-permute-start(bf16[256,128]{1,0:T(8,128)(2,1)S(1)} %get-tuple-element.972), channel_id=1, source_target_pairs={{12,0},{16,4},{20,8},{24,12},{28,16},{13,1},{17,5},{21,9},{25,13},... | collective-permute-start | bytes 196616 | tf_op jit(solution)/shard_map/ppermute | solution.py:26
  290.5 10.4 %collective-permute-start.6 = (bf16[256,128]{1,0:T(8,128)(2,1)S(1)}, bf16[256,128]{1,0:T(8,128)(2,1)S(1)}, u32[]{:S(2)}, u32[]{:S(2)}) collective-permute-start(bf16[256,128]{1,0:T(8,128)(2,1)S(1)} %get-tuple-element.971), channel_id=1, source_target_pairs={{16,0},{20,4},{24,8},{28,12},{17,1},{21,5},{25,9},{29,13},{18,2},{... | collective-permute-start | bytes 196616 | tf_op jit(solution)/shard_map/ppermute | solution.py:26
  291.8 10.4 %collective-permute-start.7 = (bf16[256,128]{1,0:T(8,128)(2,1)S(1)}, bf16[256,128]{1,0:T(8,128)(2,1)S(1)}, u32[]{:S(2)}, u32[]{:S(2)}) collective-permute-start(bf16[256,128]{1,0:T(8,128)(2,1)S(1)} %get-tuple-element.970), channel_id=1, source_target_pairs={{20,0},{24,4},{28,8},{21,1},{25,5},{29,9},{22,2},{26,6},{30,10},{2... | collective-permute-start | bytes 196616 | tf_op jit(solution)/shard_map/ppermute | solution.py:26
  292.5 10.4 %collective-permute-start.8 = (bf16[256,128]{1,0:T(8,128)(2,1)S(1)}, bf16[256,128]{1,0:T(8,128)(2,1)S(1)}, u32[]{:S(2)}, u32[]{:S(2)}) collective-permute-start(bf16[256,128]{1,0:T(8,128)(2,1)S(1)} %get-tuple-element.974), channel_id=1, source_target_pairs={{24,0},{28,4},{25,1},{29,5},{26,2},{30,6},{27,3},{31,7}} | collective-permute-start | bytes 196616 | tf_op jit(solution)/shard_map/ppermute | solution.py:26
  293.8 10.8 %collective-permute-start.10 = (bf16[256,128]{1,0:T(8,128)(2,1)S(1)}, bf16[256,128]{1,0:T(8,128)(2,1)S(1)}, u32[]{:S(2)}, u32[]{:S(2)}) collective-permute-start(bf16[256,128]{1,0:T(8,128)(2,1)S(1)} %get-tuple-element.967), channel_id=1, source_target_pairs={{8,0},{12,4},{16,8},{20,12},{24,16},{28,20},{9,1},{13,5},{17,9},{2... | collective-permute-start | bytes 196616 | tf_op jit(solution)/shard_map/ppermute | solution.py:26
  299.0 55.5 %collective-permute-start.11 = (bf16[256,128]{1,0:T(8,128)(2,1)S(1)}, bf16[256,128]{1,0:T(8,128)(2,1)S(1)}, u32[]{:S(2)}, u32[]{:S(2)}) collective-permute-start(bf16[256,128]{1,0:T(8,128)(2,1)S(1)} %get-tuple-element.966), channel_id=1, source_target_pairs={{12,0},{16,4},{20,8},{24,12},{28,16},{13,1},{17,5},{21,9},{25,13},... | collective-permute-start | bytes 196616 | tf_op jit(solution)/shard_map/ppermute | solution.py:26
  300.9 53.6 %collective-permute-start.12 = (bf16[256,128]{1,0:T(8,128)(2,1)S(1)}, bf16[256,128]{1,0:T(8,128)(2,1)S(1)}, u32[]{:S(2)}, u32[]{:S(2)}) collective-permute-start(bf16[256,128]{1,0:T(8,128)(2,1)S(1)} %get-tuple-element.965), channel_id=1, source_target_pairs={{16,0},{20,4},{24,8},{28,12},{17,1},{21,5},{25,9},{29,13},{18,2},{... | collective-permute-start | bytes 196616 | tf_op jit(solution)/shard_map/ppermute | solution.py:26
  302.2 52.3 %collective-permute-start.13 = (bf16[256,128]{1,0:T(8,128)(2,1)S(1)}, bf16[256,128]{1,0:T(8,128)(2,1)S(1)}, u32[]{:S(2)}, u32[]{:S(2)}) collective-permute-start(bf16[256,128]{1,0:T(8,128)(2,1)S(1)} %get-tuple-element.964), channel_id=1, source_target_pairs={{20,0},{24,4},{28,8},{21,1},{25,5},{29,9},{22,2},{26,6},{30,10},{2... | collective-permute-start | bytes 196616 | tf_op jit(solution)/shard_map/ppermute | solution.py:26
  302.9 51.6 %collective-permute-start.14 = (bf16[256,128]{1,0:T(8,128)(2,1)S(1)}, bf16[256,128]{1,0:T(8,128)(2,1)S(1)}, u32[]{:S(2)}, u32[]{:S(2)}) collective-permute-start(bf16[256,128]{1,0:T(8,128)(2,1)S(1)} %get-tuple-element.968), channel_id=1, source_target_pairs={{24,0},{28,4},{25,1},{29,5},{26,2},{30,6},{27,3},{31,7}} | collective-permute-start | bytes 196616 | tf_op jit(solution)/shard_map/ppermute | solution.py:26
  304.6 49.9 %collective-permute-start.9 = (bf16[256,128]{1,0:T(8,128)(2,1)S(1)}, bf16[256,128]{1,0:T(8,128)(2,1)S(1)}, u32[]{:S(2)}, u32[]{:S(2)}) collective-permute-start(bf16[256,128]{1,0:T(8,128)(2,1)S(1)} %get-tuple-element.963), channel_id=1, source_target_pairs={{4,0},{8,4},{12,8},{16,12},{20,16},{24,20},{28,24},{5,1},{9,5},{13... | collective-permute-start | bytes 196616 | tf_op jit(solution)/shard_map/ppermute | solution.py:26
  (19 other events, 46.4 us)
